TPU v7x, 512 devices: a whole 4x4x16 slice. The times are simulated.
512 devices in a mesh: lat: 16 (over x, z_hi, core), lon: 32 (over y, z_lo).
Axes of the slice: x: 4, y: 4, z: 16 (z_hi: 2, z_lo: 8; z = z_hi * 8 + z_lo), core: 2. Of those that a mesh axis runs over, the one named last changes fastest.
Arguments:
- latent: bfloat16 [256, 512, 641], P('lat', 'lon'), may hold values from -6 to 6
- filters: bfloat16 [9, 256, 9, 33], P(None, 'lat'), may hold values from -0.59765625 to 0.59765625
- widths: int32 [256, 9], P('lat'), may hold values from 0 to 16, as said below
- mix_weight: bfloat16 [9, 641, 512], P(None, None, ('lat', 'lon')), may hold values from -0.078125 to 0.078125
- mix_bias: float32 [512], replicated, may hold values from -3 to 3
Outputs:
- convolved: bfloat16 [256, 512, 512], P('lat', 'lon')
Inputs may be any that keep to these rules, and one draw needn't show every extreme that they name: widths grow toward the poles and are at most 16, reached in rows next to a pole.
All inputs are finite; a program needn't handle non-finite values.
Results may differ from a plain program's by a relative error of at most 0.0048.
Values may be sent and summed in bfloat16 or wider, within the bound.
A program may use at most 64 MiB of HBM per device.

v0:
```python
import jax
import jax.numpy as jnp
from jax import lax
from jax.sharding import PartitionSpec as P

RADIUS = 4
LON_REACH = 16


def padded(cells, sides, width, closed):
    for axis, dim in sides:
        count = lax.axis_size(axis)
        ends = count if closed else count - 1
        head = lax.slice_in_dim(cells, 0, width, axis=dim)
        tail = lax.slice_in_dim(cells, cells.shape[dim] - width, cells.shape[dim], axis=dim)
        cells = jnp.concatenate(
            [
                lax.ppermute(tail, axis, [(i, (i + 1) % count) for i in range(ends)]),
                cells,
                lax.ppermute(head, axis, [((i + 1) % count, i) for i in range(ends)]),
            ],
            axis=dim,
        )
    return cells


def passed_along(block, axis, distance):
    devices = range(lax.axis_size(axis))
    route = [((i - distance) % len(devices), i) for i in devices]
    return lax.ppermute(block, axis, route)


def mend_poles(banded, polar_pair, lat_index, lat_count):
    upper_rim = jnp.where(lat_index == 0, polar_pair[0], banded[:RADIUS])
    lower_rim = jnp.where(lat_index == lat_count - 1, polar_pair[1], banded[-RADIUS:])
    return jnp.concatenate([upper_rim, banded[RADIUS:-RADIUS], lower_rim], 0)


def body(latent, filters, widths, mix_weight, mix_bias):
    lat_count = lax.axis_size("lat")
    lon_count = lax.axis_size("lon")
    lat_index = lax.axis_index("lat")
    banded = padded(latent, (("lat", 0),), RADIUS, False)
    polar_pair = passed_along(
        (latent[:RADIUS][::-1], latent[-RADIUS:][::-1]), "lon", lon_count // 2
    )
    banded = mend_poles(banded, polar_pair, lat_index, lat_count)
    extended = padded(banded, (("lon", 1),), LON_REACH, True)
    lat_dev, lon_dev, channels = latent.shape
    stencil_span = 2 * LON_REACH + 1
    lookup_table_shape = (lon_dev, lon_dev + 2 * LON_REACH, stencil_span)
    column = lax.broadcasted_iota(jnp.int32, lookup_table_shape, 0)
    source = lax.broadcasted_iota(jnp.int32, lookup_table_shape, 1)
    offset = lax.broadcasted_iota(jnp.int32, lookup_table_shape, 2)
    basis_selector = (source == column + offset).astype(jnp.bfloat16)
    shifts = jnp.arange(stencil_span, dtype=jnp.int32) - LON_REACH
    inside = jnp.abs(shifts)[None, None, :] <= widths[:, :, None]
    coefficients = jnp.where(inside[None], filters, jnp.zeros((), filters.dtype))
    per_row = jnp.transpose(coefficients, (1, 0, 2, 3))

    def one_row(packed):
        row_coefficient, row_index = packed
        banded_matrix = jnp.einsum(
            "blw,ocw->bolc", row_coefficient, basis_selector, preferred_element_type=jnp.float32
        ).astype(jnp.bfloat16)
        slab_rows = lax.dynamic_slice_in_dim(extended, row_index, 2 * RADIUS + 1, 0)
        return jnp.einsum(
            "kjdp,dpc->kjc", banded_matrix, slab_rows, preferred_element_type=jnp.float32
        ).astype(jnp.bfloat16)

    features = lax.map(one_row, (per_row, jnp.arange(lat_dev, dtype=jnp.int32)))
    channel_mixed_output = lax.dot_general(
        features,
        lax.all_gather(mix_weight, ("lat", "lon"), axis=2, tiled=True),
        (((1, 3), (0, 1)), ((), ())),
        preferred_element_type=jnp.float32,
    )
    return jax.nn.gelu(channel_mixed_output + mix_bias, approximate=False).astype(jnp.bfloat16)


def solution(mesh):
    placed = (
        P("lat", "lon", None),
        P(None, "lat", None, None),
        P("lat", None),
        P(None, None, ("lat", "lon")),
        P(),
    )
    return jax.shard_map(
        body, mesh=mesh, in_specs=placed, out_specs=P("lat", "lon", None), check_vma=False
    )
```

profile of v0, /device:TPU:1, one launch (start us, length us, event | category | flops | bytes accessed | tf_op | source)
XLA Modules:
  0.0 1480.2 jit_solution(731969707399384717)
XLA Ops:
  6.5 0.7 all-gather.2.cloned.1.call-update
  7.3 1.0 fusion.39
  8.2 5.6 collective-permute-start.2
  13.9 5.0 collective-permute-start.3
  18.9 13.2 collective-permute-start.1
  32.1 2.0 collective-permute-start
  34.1 5.0 collective-permute-done
  39.1 1.1 pad_maximum_fusion.1
  40.2 2.6 collective-permute-start.4
  42.9 11.4 collective-permute-start.5
  54.2 0.8 broadcast_compare_fusion
  55.1 1.1 fusion.26
  56.1 9.7 collective-permute-done.4
  66.0 1.2 pad_maximum_fusion
  67.3 66.9 %while.11 = (s32[]{:T(128)}, bf16[16,9,16,641]{3,2,1,0:T(8,128)(2,1)}, bf16[16,9,9,33]{3,2,1,0:T(8,128)(2,1)S(1)}, s32[16]{0:T(128)S(1)}, bf16[24,48,641]{2,1,0:...) while((s32[]{:T(128)}, bf16[16,9,16,641]{3,2,1,0:T(8,128)(2,1)}, ...), condition=%wide.region_1.2_spmd.clone, body=%wide.region_0.1_spmd.clone.sunk | while | flops 84024720 | bytes 1636491 | solution.py:71
  67.3 0.7 dynamic_slice.27
  70.4 1.0 fusion.52
  71.4 0.7 dynamic_slice.27
  74.6 1.1 fusion.52
  75.7 0.7 dynamic_slice.27
  78.8 1.1 fusion.52
  79.8 0.7 dynamic_slice.27
  83.0 1.1 fusion.52
  84.0 0.7 dynamic_slice.27
  87.2 1.1 fusion.52
  88.2 0.7 dynamic_slice.27
  91.3 1.0 fusion.52
  92.4 0.7 dynamic_slice.27
  95.5 1.1 fusion.52
  96.5 0.7 dynamic_slice.27
  99.7 1.0 fusion.52
  100.7 0.7 dynamic_slice.27
  103.8 1.0 fusion.52
  104.9 0.7 dynamic_slice.27
  108.0 1.1 fusion.52
  109.1 0.7 dynamic_slice.27
  112.2 1.1 fusion.52
  113.3 0.7 dynamic_slice.27
  116.4 1.1 fusion.52
  117.5 0.7 dynamic_slice.27
  120.6 1.1 fusion.52
  124.8 1.0 fusion.52
  125.8 0.7 dynamic_slice.27
  128.9 1.0 fusion.52
  130.0 0.7 dynamic_slice.27
  133.1 1.0 fusion.52
  134.1 1327.7 %all-gather.2.cloned.1.call-done = bf16[9,641,512]{1,0,2:T(8,128)(2,1)} async-done(((bf16[9,641,1]{1,0,2:T(8,128)(2,1)}), bf16[9,641,512]{1,0,2:T(8,128)(2,1)}) %all-gather.2.cloned.1.call-update) | async-done | bytes 5907472 | tf_op jit(solution)/shard_map/all_gather | solution.py:74
  1461.9 11.5 fusion.29
  (33 shorter events, 7.0 us)
Async XLA Ops:
  6.5 59.5 %copy-start = (bf16[16,16,641]{2,1,0:T(8,128)(2,1)S(1)}, bf16[16,16,641]{2,1,0:T(8,128)(2,1)}, u32[]{:S(2)}) copy-start(bf16[16,16,641]{2,1,0:T(8,128)(2,1)} %param.7) | copy-start | bytes 984580
  6.5 1455.4 %all-gather.2.cloned.1.call-start = ((), (), s32[]{:S(2)}) async-start(), calls=%async_computation | async-start | bytes 12607488 | tf_op jit(solution)/shard_map/all_gather | solution.py:74
  8.2 25.9 %collective-permute-start.2 = (bf16[4,16,641]{2,1,0:T(8,128)(2,1)S(1)}, bf16[4,16,641]{2,1,0:T(8,128)(2,1)S(1)}, u32[]{:S(2)}, u32[]{:S(2)}) collective-permute-start(bf16[4,16,641]{2,1,0:T(8,128)(2,1)S(1)} %rev.7), channel_id=1, source_target_pairs={{16,0},{17,1},{18,2},{19,3},{20,4},{21,5},{22,6},{23,7},{24,8},{25... | collective-permute-start | bytes 246152 | tf_op jit(solution)/shard_map/ppermute | solution.py:30
  13.9 20.2 %collective-permute-start.3 = (bf16[4,16,641]{2,1,0:T(8,128)(2,1)S(1)}, bf16[4,16,641]{2,1,0:T(8,128)(2,1)S(1)}, u32[]{:S(2)}, u32[]{:S(2)}) collective-permute-start(bf16[4,16,641]{2,1,0:T(8,128)(2,1)S(1)} %get-tuple-element.60), channel_id=1, source_target_pairs={{32,0},{64,32},{96,64},{128,96},{160,128},{192,160},{224,192},{256... | collective-permute-start | bytes 246152 | tf_op jit(solution)/shard_map/ppermute | solution.py:20
  18.9 20.2 %collective-permute-start.1 = (bf16[4,16,641]{2,1,0:T(8,128)(2,1)S(1)}, bf16[4,16,641]{2,1,0:T(8,128)(2,1)S(1)}, u32[]{:S(2)}, u32[]{:S(2)}) collective-permute-start(bf16[4,16,641]{2,1,0:T(8,128)(2,1)S(1)} %get-tuple-element.61), channel_id=1, source_target_pairs={{0,32},{32,64},{64,96},{96,128},{128,160},{160,192},{192,224},{224... | collective-permute-start | bytes 246152 | tf_op jit(solution)/shard_map/ppermute | solution.py:18
  32.1 7.0 collective-permute-start
  40.2 25.7 %collective-permute-start.4 = (bf16[24,16,641]{2,1,0:T(8,128)(2,1)S(1)}, bf16[24,16,641]{2,1,0:T(8,128)(2,1)S(1)}, u32[]{:S(2)}, u32[]{:S(2)}) collective-permute-start(bf16[24,16,641]{2,1,0:T(8,128)(2,1)S(1)} %pad_maximum_fusion.1), channel_id=1, source_target_pairs={{0,1},{1,2},{2,3},{3,4},{4,5},{5,6},{6,7},{7,8},{8,9},{9,10},{10,1... | collective-permute-start | bytes 1476872 | tf_op jit(solution)/shard_map/ppermute | solution.py:18
  42.9 23.1 %collective-permute-start.5 = (bf16[24,16,641]{2,1,0:T(8,128)(2,1)S(1)}, bf16[24,16,641]{2,1,0:T(8,128)(2,1)}, u32[]{:S(2)}, u32[]{:S(2)}) collective-permute-start(bf16[24,16,641]{2,1,0:T(8,128)(2,1)S(1)} %pad_maximum_fusion.1), channel_id=1, source_target_pairs={{1,0},{2,1},{3,2},{4,3},{5,4},{6,5},{7,6},{8,7},{9,8},{10,9},{11,1... | collective-permute-start | bytes 1476872 | tf_op jit(solution)/shard_map/ppermute | solution.py:20
  67.2 1394.7 %copy-start.1 = (f32[512]{0:T(512)S(1)}, f32[512]{0:T(512)}, u32[]{:S(2)}) copy-start(f32[512]{0:T(512)} %param.11) | copy-start | bytes 6148
Sparse Core Ops, SparseCore 0:
  9.6 1452.2 all-gather.1
where the time goes:
time: 1490 us; the launch traced here: 1480 us
  waiting for transfers between devices  1340 us (90%)
  starting transfers between devices  39.8 us (3%)
  matrix products  34.5 us (2%)
  loops' own time  33.4 us (2%)
    all_gather x1, waiting for transfers between devices, body(): lax.all_gather(mix_weight, ('lat', 'lon'), axis=2, tiled=True)  1330 us
    another operation x1, loops' own time, body(): features = lax.map(one_row, (per_row, jnp.arange(lat_dev, dtype=jnp.int32)))  33.4 us
  transfers between devices with their start and end apart: 7, of which 4 were waited for; matrix products, arithmetic and copies ran while one was open for 3% of the time, Pallas kernels for 0%

commit v1 on v0

v1 whole, which is shorter than its diff:
```python
import math

import jax
import jax.numpy as jnp
from jax import lax
from jax.experimental import pallas as pl
from jax.experimental.pallas import tpu as pltpu
from jax.sharding import PartitionSpec as P

RADIUS = 4
REACH = 16
BASES = 9
MAIN = 640
SPAN = 48
MESH = pl.DeviceIdType.MESH
BF = jnp.bfloat16
F32 = jnp.float32

Z1, P1, H1, P2, H2, DD = range(6)


def device_of(x, y, z, core):
    return (x * 4 + (z // 8) * 2 + core, y * 8 + z % 8)


def build_rows(coef_ref, a_ref, pair):
    lane = lax.broadcasted_iota(jnp.int32, (16, 128), 1)
    zero = jnp.zeros((16, 128), F32)
    for s in range(2):
        for k in range(BASES):
            taps = coef_ref[pair * 2 + s, k].astype(F32)
            taps = jnp.pad(taps, ((0, 0), (0, 128 - taps.shape[1])))
            tiles = [None] * 4

            def put(t, part):
                tiles[t] = part if tiles[t] is None else tiles[t] + part

            for d in range(2 * RADIUS + 1):
                first, at = divmod(SPAN * (d + s), 128)
                line = jnp.broadcast_to(taps[d : d + 1], (16, 128))
                line = pltpu.roll(line, at, 1, stride=1, stride_axis=0)
                if at + SPAN > 128:
                    put(first, jnp.where(lane >= at, line, zero))
                    put(first + 1, jnp.where(lane < at, line, zero))
                else:
                    put(first, line)
            rows = pl.ds((s * BASES + k) * 16, 16)
            a_ref[pair, rows, :] = jnp.concatenate(tiles, 1).astype(BF)


def stencil_rows(a_ref, e_ref, f_ref, pair):
    lane = lax.broadcasted_iota(jnp.int32, (16, 128), 1)
    slab = e_ref[pl.ds(pair * 2, 10)].reshape(10 * SPAN, MAIN + 1)
    found = jnp.dot(a_ref[pair][:, : 10 * SPAN], slab, preferred_element_type=F32)
    for s in range(2):
        rows = pl.ds(pl.multiple_of((pair * 2 + s) * 16, 16), 16)
        last = jnp.zeros((16, 128), F32)
        for k in range(BASES):
            part = found[(s * BASES + k) * 16 : (s * BASES + k + 1) * 16]
            f_ref[rows, k * MAIN : (k + 1) * MAIN] = part[:, :MAIN].astype(BF)
            last = jnp.where(lane == k, jnp.broadcast_to(part[:, MAIN:], (16, 128)), last)
        f_ref[rows, BASES * MAIN :] = last.astype(BF)


def body_kernel(
    w_in, latent, coef_ref, bias_ref, out_ref,
    g_ref, e_ref, a_ref, f_ref, wt_ref,
    send, recv, hsend, hrecv, rsend, rrecv, own_sem,
):
    lat, lon = lax.axis_index("lat"), lax.axis_index("lon")
    x, core = lat // 4, lat % 2
    y = lon // 8
    z = ((lat // 2) % 2) * 8 + lon % 8
    xs = ((x + 3) % 4, (x + 1) % 4)
    ys = ((y + 3) % 4, (y + 1) % 4)
    zs = ((z + 15) % 16, (z + 1) % 16)
    to_x = [device_of(v, y, z, core) for v in xs]
    to_y = [device_of(x, v, z, core) for v in ys]
    to_z = [device_of(x, y, v, core) for v in zs]
    sibling = (lat + 1 - 2 * core, lon)
    to_lon = [(lat, (lon + 31) % 32), (lat, (lon + 1) % 32)]
    top, bottom = lat == 0, lat == 15
    opposite = (lon + 16) % 32
    up = (jnp.where(top, 0, lat - 1), jnp.where(top, opposite, lon))
    down = (jnp.where(bottom, 15, lat + 1), jnp.where(bottom, opposite, lon))

    barrier = pltpu.get_barrier_semaphore()
    peers = to_x + to_y + to_z + [sibling] + to_lon + [up, down]
    for peer in peers:
        pl.semaphore_signal(barrier, inc=1, device_id=peer, device_id_type=MESH)
    pl.semaphore_wait(barrier, len(peers))

    def remote(src, dst, s, r, where):
        return pltpu.make_async_remote_copy(
            src_ref=src, dst_ref=dst, send_sem=s, recv_sem=r,
            device_id=where, device_id_type=MESH,
        )

    def column(part, side):
        begin, size = ((RADIUS, 16), (0, RADIUS), (RADIUS + 16, RADIUS))[part]
        src = latent if part == 0 else e_ref.at[pl.ds(begin, size), pl.ds(16, 16), :]
        dst = e_ref.at[pl.ds(begin, size), pl.ds(32 * (1 - side), 16), :]
        return remote(src, dst, hsend.at[part, side], hrecv.at[part, side], to_lon[side])

    def strip(edge, q):
        pole = top if edge == 0 else bottom
        row = jnp.where(pole, 3 - q, 20 + q) if edge == 0 else jnp.where(pole, 23 - q, q)
        slot = jnp.where(pole, edge, 1 - edge)
        return remote(
            latent.at[edge * 12 + q], e_ref.at[row, pl.ds(16, 16), :],
            rsend.at[edge, q], rrecv.at[slot], down if edge else up,
        )

    for q in range(RADIUS):
        strip(0, q).start()
        strip(1, q).start()
    for side in range(2):
        column(0, side).start()

    def block(zb):
        return g_ref.at[x, zb // 8, core, y, zb % 8]

    own_w = pltpu.make_async_copy(w_in, block(z), own_sem.at[0])
    own_w.start()
    own_e = pltpu.make_async_copy(
        latent, e_ref.at[pl.ds(RADIUS, 16), pl.ds(16, 16), :], own_sem.at[1]
    )
    own_e.start()

    def z_copy(zb, b, side, src=None):
        return remote(
            block(zb) if src is None else src, block(zb),
            send.at[Z1, b, 0], recv.at[Z1, b, 0], to_z[side],
        )

    z_copy(z, 2, 0, w_in).start()
    z_copy(z, 1, 1, w_in).start()
    own_w.wait()

    def pieces(i, odd):
        b = 2 * i + odd
        zb = (z + 15 - i) % 16 if odd else (z + i) % 16
        hi, lo = zb // 8, zb % 8
        near, far = (ys, xs) if odd else (xs, ys)
        to_near, to_far = (to_y, to_x) if odd else (to_x, to_y)

        def one(v, rows=None):
            ref = g_ref.at[x, hi, core, v, lo] if odd else g_ref.at[v, hi, core, y, lo]
            return ref if rows is None else ref.at[rows]

        def line(v, part=slice(None)):
            return g_ref.at[v, hi, core, part, lo] if odd else g_ref.at[part, hi, core, v, lo]

        me = (y, x) if odd else (x, y)
        halves = (pl.ds(0, 24), pl.ds(24, 24))
        pairs = (pl.ds(0, 2), pl.ds(2, 2))

        def sem(stage, side):
            return send.at[stage, b, side], recv.at[stage, b, side]

        def copies(stage, side, incoming=False):
            if stage == P1:
                v = near[side] if incoming else me[0]
                return remote(one(v), one(v), *sem(P1, 1 - side if incoming else side), to_near[side])
            if stage == H1:
                far_one = (me[0] + 2) % 4
                s = 1 - side if incoming else side
                v = far_one if incoming else near[1 - side]
                rows = halves[0] if s == 1 else halves[1]
                return remote(one(v, rows), one(v, rows), *sem(H1, s), to_near[side])
            if stage == P2:
                v = far[side] if incoming else me[1]
                return remote(line(v), line(v), *sem(P2, 1 - side if incoming else side), to_far[side])
            far_line = (me[1] + 2) % 4
            s = 1 - side if incoming else side
            v = far_line if incoming else far[1 - side]
            part = pairs[0] if s == 1 else pairs[1]
            return remote(line(v, part), line(v, part), *sem(H2, s), to_far[side])

        def plane():
            src = g_ref.at[:, hi, core, :, lo]
            return remote(src, src, send.at[DD, b, 0], recv.at[DD, b, 0], sibling)

        return b, zb, copies, plane

    def from_sibling(i, odd):
        b = 2 * i + odd
        zb = (z + 15 - i) % 16 if odd else (z + i) % 16
        dst = g_ref.at[:, zb // 8, 1 - core, :, zb % 8]
        return remote(dst, dst, send.at[DD, b, 0], recv.at[DD, b, 0], sibling)

    def step(t, carry):
        @pl.when(t < 8)
        def _():
            for odd in range(2):
                b, zb, copies, _ = pieces(t, odd)

                def arrive():
                    z_copy(zb, b, 0).wait_recv()

                if odd:
                    arrive()
                else:
                    pl.when(t > 0)(arrive)

                @pl.when((t < 7) & (t > 0) if not odd else t < 7)
                def _():
                    z_copy(zb, b + 2, odd).start()

                for side in range(2):
                    copies(P1, side).start()

        @pl.when((t >= 1) & (t < 9))
        def _():
            for odd in range(2):
                _, _, copies, _ = pieces(t - 1, odd)
                for side in range(2):
                    copies(P1, 1 - side, True).wait_recv()
                    copies(H1, side).start()

        @pl.when((t >= 2) & (t < 10))
        def _():
            for odd in range(2):
                _, _, copies, _ = pieces(t - 2, odd)
                for side in range(2):
                    copies(H1, side, True).wait_recv()
                for side in range(2):
                    copies(P2, side).start()

        @pl.when((t >= 3) & (t < 11))
        def _():
            for odd in range(2):
                _, _, copies, _ = pieces(t - 3, odd)
                for side in range(2):
                    copies(P2, 1 - side, True).wait_recv()
                    copies(H2, side).start()

        @pl.when(t >= 4)
        def _():
            for odd in range(2):
                _, _, copies, plane = pieces(t - 4, odd)
                for side in range(2):
                    copies(H2, side, True).wait_recv()
                plane().start()

        @pl.when(t < 8)
        def _():
            build_rows(coef_ref, a_ref, t)

        @pl.when(t == 5)
        def _():
            for part in (1, 2):
                rows = e_ref.at[pl.ds((0, 20)[part - 1], RADIUS), pl.ds(16, 16), :]
                pltpu.make_async_copy(rows, rows, rrecv.at[part - 1]).wait()
                for side in range(2):
                    column(part, side).start()

        return carry

    lax.fori_loop(0, 12, step, 0)

    own_e.wait()
    for part in range(3):
        for side in range(2):
            column(part, side).wait_recv()

    def features(pair, carry):
        stencil_rows(a_ref, e_ref, f_ref, pair)
        return carry

    lax.fori_loop(0, 8, features, 0)

    def wait_planes(i, carry):
        for odd in range(2):
            from_sibling(i, odd).wait_recv()
        return carry

    lax.fori_loop(0, 8, wait_planes, 0)

    def lay(n, carry):
        band, half = n // 2, n % 2
        rows = g_ref[band // 4, (band // 2) % 2, band % 2, pl.ds(half * 2, 2)]
        flat = rows.reshape(16, 48 * 128)
        wt_ref[pl.ds(pl.multiple_of(n * 16, 16), 16), :] = flat[:, : 46 * 128]
        return carry

    lax.fori_loop(0, 32, lay, 0)

    def mix(n, carry):
        cols = pl.ds(pl.multiple_of(n * 256, 256), 256)
        total = lax.dot_general(
            f_ref[...], wt_ref[cols, :], (((1,), (1,)), ((), ())), preferred_element_type=F32
        )
        total = total + bias_ref[:, cols]
        value = 0.5 * total * (1.0 + lax.erf(total * math.sqrt(0.5)))
        out_ref[:, cols] = value.astype(BF)
        return carry

    lax.fori_loop(0, 2, mix, 0)

    def drain(i, carry):
        for odd in range(2):
            b, zb, copies, plane = pieces(i, odd)

            @pl.when((i > 0) if not odd else (i >= 0))
            def _():
                z_copy(zb, b, 0).wait_send()

            for stage in (P1, H1, P2, H2):
                for side in range(2):
                    copies(stage, side).wait_send()
            plane().wait_send()
        return carry

    lax.fori_loop(0, 8, drain, 0)
    for q in range(RADIUS):
        strip(0, q).wait_send()
        strip(1, q).wait_send()
    for part in range(3):
        for side in range(2):
            column(part, side).wait_send()


def body(latent, filters, widths, mix_weight, mix_bias):
    shifts = jnp.arange(2 * REACH + 1, dtype=jnp.int32) - REACH
    inside = jnp.abs(shifts)[None, None, :] <= widths[:, :, None]
    coefficients = jnp.where(inside[None], filters, jnp.zeros((), filters.dtype))
    coefficients = jnp.transpose(coefficients, (1, 0, 2, 3))
    weight = mix_weight[:, :, 0]
    packed = jnp.concatenate(
        [
            weight[:, :MAIN].reshape(45, 128),
            jnp.pad(weight[:, MAIN], (0, 128 - BASES))[None],
            jnp.zeros((2, 128), BF),
        ]
    )
    vmem = pl.BlockSpec(memory_space=pltpu.VMEM)
    dma = pltpu.SemaphoreType.DMA
    out = pl.pallas_call(
        body_kernel,
        out_shape=jax.ShapeDtypeStruct((256, 512), BF),
        in_specs=[vmem] * 4,
        out_specs=vmem,
        scratch_shapes=[
            pltpu.VMEM((4, 2, 2, 4, 8, 48, 128), BF),
            pltpu.VMEM((24, SPAN, MAIN + 1), BF),
            pltpu.VMEM((8, 288, 512), BF),
            pltpu.VMEM((256, 46 * 128), BF),
            pltpu.VMEM((512, 46 * 128), BF),
            dma((6, 16, 2)),
            dma((6, 16, 2)),
            dma((3, 2)),
            dma((3, 2)),
            dma((2, RADIUS)),
            dma((2,)),
            dma((2,)),
        ],
        compiler_params=pltpu.CompilerParams(
            collective_id=0, has_side_effects=True, vmem_limit_bytes=60 << 20
        ),
        name="sphere",
    )(packed, latent, coefficients, mix_bias[None])
    return out.reshape(16, 16, 512)


def solution(mesh):
    placed = (
        P("lat", "lon", None),
        P(None, "lat", None, None),
        P("lat", None),
        P(None, None, ("lat", "lon")),
        P(),
    )
    return jax.shard_map(
        body, mesh=mesh, in_specs=placed, out_specs=P("lat", "lon", None), check_vma=False
    )
```

time: 1490 us -> 100 us (0.07)
  the two profiles are of different devices: /device:TPU:1 before, /device:TPU:32 now
where the time goes in v1:
time: 100 us; the launch traced here: 99.9 us
  Pallas kernels  93.9 us (94%)
  local copies, waits for them, and re-layouts  3.33 us (3%)
  other arithmetic  2.67 us (3%)
    pallas_call x1, Pallas kernels, body(): pl.pallas_call(body_kernel, out_shape=jax.ShapeDtypeStruct((256, 512), BF...  93.9 us

profile of v1, /device:TPU:32, one launch (start us, length us, event | category | flops | bytes accessed | tf_op | source)
XLA Modules:
  0.0 99.9 jit_solution(5611572978819977309)
XLA Ops:
  0.0 0.8 slice_reduce_fusion
  0.8 0.1 pad.7.clone
  0.9 0.7 slice.8
  1.7 0.0 copy-start
  1.7 0.7 maximum_maximum_fusion.w_in
  2.4 0.0 copy-done
  2.4 0.1 broadcast_compare_fusion
  2.5 1.9 %fusion.coef_ref = bf16[16,9,9,33]{3,2,1,0:T(8,128)(2,1)} fusion(bf16[9,16,9,33]{3,1,2,0:T(8,128)(2,1)} %param.6, pred[16,9,33]{2,1,0:T(8,128)(4,1)S(1)} %broadcast_compare_fusion), kind=kLoop, calls=%fused_computation.1 | loop fusion | flops 42768 | bytes 175824 | tf_op jit(solution)/shard_map/transpose | solution.py:328
  4.4 93.9 %sphere.1 = bf16[256,512]{1,0:T(8,128)(2,1)} custom-call(bf16[48,128]{1,0:T(8,128)(2,1)} %maximum_maximum_fusion.w_in, bf16[16,16,641]{2,1,0:T(8,128)(2,1)} %latent.1, bf16[16,9,9,33]{3,2,1,0:T(8,128)(2,1)} %fusion.coef_ref, f32[1,512]{1,0:T(1,128)} %bitcast.10), custom_call_target="tpu_custom_call" | custom-call | tf_op jit(solution)/shard_map/sphere/pallas_call | solution.py:339
  98.2 1.7 %copy.12 = bf16[16,16,512]{2,1,0:T(8,128)(2,1)} copy(bf16[16,16,512]{2,1,0:T(8,128)(2,1)} %bitcast.7) | data formatting | bytes 524288
  (4 shorter events, 0.0 us)
Async XLA Ops:
  1.7 0.7 copy-start

commit v2 on v1

v2 whole, which is shorter than its diff:
```python
import math

import jax
import jax.numpy as jnp
from jax import lax
from jax.experimental import pallas as pl
from jax.experimental.pallas import tpu as pltpu
from jax.sharding import PartitionSpec as P

RADIUS = 4
REACH = 16
BASES = 9
MAIN = 640
SPAN = 48
DEPTH = 46 * 128
MESH = pl.DeviceIdType.MESH
BF = jnp.bfloat16
F32 = jnp.float32

Z1, P1, P2, H2, DD = range(5)
OWN, OUTER, INNER = range(3)


def device_of(x, y, z, core):
    return (x * 4 + (z // 8) * 2 + core, y * 8 + z % 8)


def prepare_kernel(w_ref, tail_ref, packed_ref, extra_ref, rows_ref):
    w = w_ref[0].astype(F32)
    for t in range(5):
        rows_ref[t * BASES : (t + 1) * BASES, :] = w[:, t * 128 : (t + 1) * 128]
    lane = lax.broadcasted_iota(jnp.int32, (BASES, 128), 1)
    row = lax.broadcasted_iota(jnp.int32, (BASES, 128), 0)
    last = jnp.where(lane == row, jnp.broadcast_to(w[:, MAIN:], (BASES, 128)), 0.0)
    rows_ref[45:46, :] = jnp.sum(last, axis=0, keepdims=True)
    rows_ref[46:48, :] = jnp.zeros((2, 128), F32)
    packed_ref[...] = rows_ref[...].astype(BF)
    lane = lax.broadcasted_iota(jnp.int32, (16, 128), 1)
    extra = jnp.zeros((16, 128), F32)
    for r in range(16):
        column = tail_ref[r, :, 0:1].astype(F32)
        extra = jnp.where(lane == RADIUS + r, jnp.broadcast_to(column, (16, 128)), extra)
    extra_ref[...] = extra.astype(BF)


def mask_taps(filters_ref, widths_ref, taps_ref):
    lane = lax.broadcasted_iota(jnp.int32, (16, 128), 1)
    inside = [
        jnp.abs(lane - REACH) <= jnp.broadcast_to(widths_ref[:, d : d + 1], (16, 128))
        for d in range(2 * RADIUS + 1)
    ]
    for k in range(BASES):
        taps = filters_ref[k].astype(F32)
        taps = jnp.pad(taps, ((0, 0), (0, 0), (0, 128 - taps.shape[2])))
        taps = jnp.stack([jnp.where(inside[d], taps[d], 0.0) for d in range(2 * RADIUS + 1)])
        taps_ref[k] = jnp.transpose(taps, (1, 0, 2))


def build_rows(taps_ref, a_ref, pair):
    lane = lax.broadcasted_iota(jnp.int32, (16, 128), 1)
    zero = jnp.zeros((16, 128), F32)
    for s in range(2):
        i = pair * 2 + s
        for k in range(BASES):
            taps = taps_ref[k, i]
            tiles = [None] * 4

            def put(t, part):
                tiles[t] = part if tiles[t] is None else tiles[t] + part

            for d in range(2 * RADIUS + 1):
                first, at = divmod(SPAN * (d + s), 128)
                line = jnp.broadcast_to(taps[d : d + 1], (16, 128))
                line = pltpu.roll(line, at, 1, stride=1, stride_axis=0)
                if at + SPAN > 128:
                    put(first, jnp.where(lane >= at, line, zero))
                    put(first + 1, jnp.where(lane < at, line, zero))
                else:
                    put(first, line)
            rows = pl.ds((s * BASES + k) * 16, 16)
            a_ref[pair, rows, :] = jnp.concatenate(tiles, 1).astype(BF)


def stencil_rows(a_ref, e_ref, f_ref, pair):
    lane = lax.broadcasted_iota(jnp.int32, (16, 128), 1)
    slab = e_ref[pl.ds(pair * 2, 10)].reshape(10 * SPAN, MAIN + 128)
    found = jnp.dot(a_ref[pair][:, : 10 * SPAN], slab, preferred_element_type=F32)
    for s in range(2):
        rows = pl.ds(pl.multiple_of((pair * 2 + s) * 16, 16), 16)
        last = jnp.zeros((16, 128), F32)
        for k in range(BASES):
            part = found[(s * BASES + k) * 16 : (s * BASES + k + 1) * 16]
            for t in range(5):
                h = t * BASES + k
                f_ref[rows, h * 128 : (h + 1) * 128] = part[:, t * 128 : (t + 1) * 128].astype(BF)
            tail = jnp.sum(part[:, MAIN:], axis=1, keepdims=True)
            last = jnp.where(lane == k, jnp.broadcast_to(tail, (16, 128)), last)
        f_ref[rows, 45 * 128 :] = last.astype(BF)


def main_kernel(
    w_in, extra, latent, filters_ref, widths_ref, bias_ref, out_ref,
    g_ref, e_ref, x_ref, taps_ref, a_ref, f_ref, wt_ref,
    send, recv, csend, crecv, xsend, xrecv, osend, orecv, own_sem,
):
    lat, lon = lax.axis_index("lat"), lax.axis_index("lon")
    x, core = lat // 4, lat % 2
    y = lon // 8
    z = ((lat // 2) % 2) * 8 + lon % 8
    xs = ((x + 3) % 4, (x + 1) % 4, (x + 2) % 4)
    ys = ((y + 3) % 4, (y + 1) % 4, (y + 2) % 4)
    to_x = [device_of(v, y, z, core) for v in xs]
    to_y = [device_of(x, v, z, core) for v in ys]
    to_z = [device_of(x, y, v, core) for v in ((z + 15) % 16, (z + 1) % 16)]
    sibling = (lat + 1 - 2 * core, lon)
    to_lon = [(lat, (lon + 31) % 32), (lat, (lon + 1) % 32)]
    top, bottom = lat == 0, lat == 15
    pole = top | bottom
    beyond = (
        jnp.where(pole, lat, lat - 1 + 2 * core),
        jnp.where(pole, (lon + 16) % 32, lon),
    )

    barrier = pltpu.get_barrier_semaphore()
    peers = to_x + to_y + to_z + [sibling] + to_lon + [beyond]
    for peer in peers:
        pl.semaphore_signal(barrier, inc=1, device_id=peer, device_id_type=MESH)
    pl.semaphore_wait(barrier, len(peers))

    def remote(src, dst, s, r, where):
        return pltpu.make_async_remote_copy(
            src_ref=src, dst_ref=dst, send_sem=s, recv_sem=r,
            device_id=where, device_id_type=MESH,
        )

    main = pl.ds(0, MAIN)
    centre = pl.ds(16, 16)

    def column(n, side):
        rows = pl.ds(RADIUS + 2 * n, 2)
        dst = e_ref.at[rows, pl.ds(32 * (1 - side), 16), main]
        return remote(
            latent.at[pl.ds(2 * n, 2), :, main], dst,
            csend.at[n, side], crecv.at[n, side], to_lon[side],
        )

    def outer_column(m, side):
        rows = pl.ds(20 * core + 2 * m, 2)
        dst = e_ref.at[rows, pl.ds(32 * (1 - side), 16), main]
        return remote(
            e_ref.at[rows, centre, main], dst,
            csend.at[8 + m, side], crecv.at[8 + m, side], to_lon[side],
        )

    def strip(q):
        row = jnp.where(pole, jnp.where(core == 0, 3 - q, 23 - q), jnp.where(core == 0, 20 + q, q))
        return remote(
            latent.at[12 * core + q, :, main], e_ref.at[row, centre, main],
            osend.at[q], orecv.at[0], beyond,
        )

    def extra_beyond():
        return remote(extra, x_ref.at[OUTER, centre, :], xsend.at[2], xrecv.at[2], beyond)

    def extra_column(part, side):
        src = extra if part == OWN else x_ref.at[OUTER, centre, :]
        dst = x_ref.at[part, pl.ds(32 * (1 - side), 16), :]
        return remote(src, dst, xsend.at[3 * part + side], xrecv.at[3 * part + side], to_lon[side])

    def inner_rows():
        src = e_ref.at[pl.ds(16 - 12 * core, RADIUS), :, main]
        dst = e_ref.at[pl.ds(20 * core, RADIUS), :, main]
        return remote(src, dst, xsend.at[5], xrecv.at[5], sibling)

    def inner_extra():
        return remote(x_ref.at[OWN], x_ref.at[INNER], xsend.at[6], xrecv.at[6], sibling)

    def block(zb):
        return g_ref.at[x, zb // 8, core, y, zb % 8]

    def z_copy(zb, b, side, src=None):
        return remote(
            block(zb) if src is None else src, block(zb),
            send.at[Z1, b, 0], recv.at[Z1, b, 0], to_z[side],
        )

    z_copy(z, 2, 0, w_in).start()
    z_copy(z, 1, 1, w_in).start()
    extra_beyond().start()
    for q in range(RADIUS):
        strip(q).start()
    for side in range(2):
        extra_column(OWN, side).start()
    own = [
        pltpu.make_async_copy(w_in, block(z), own_sem.at[0]),
        pltpu.make_async_copy(
            latent.at[:, :, main], e_ref.at[pl.ds(RADIUS, 16), centre, main], own_sem.at[1]
        ),
        pltpu.make_async_copy(extra, x_ref.at[OWN, centre, :], own_sem.at[2]),
    ]
    for copy in own:
        copy.start()
    own[0].wait()
    mask_taps(filters_ref, widths_ref, taps_ref)

    def pieces(i, odd):
        b = 2 * i + odd
        zb = (z + 15 - i) % 16 if odd else (z + i) % 16
        hi, lo = zb // 8, zb % 8
        near, far = (ys, xs) if odd else (xs, ys)
        to_near, to_far = (to_y, to_x) if odd else (to_x, to_y)
        me = (y, x) if odd else (x, y)
        pairs = (pl.ds(0, 2), pl.ds(2, 2))

        def one(v):
            return g_ref.at[x, hi, core, v, lo] if odd else g_ref.at[v, hi, core, y, lo]

        def line(v, part=slice(None)):
            return g_ref.at[v, hi, core, part, lo] if odd else g_ref.at[part, hi, core, v, lo]

        def sem(stage, slot):
            return send.at[stage, b, slot], recv.at[stage, b, slot]

        def copies(stage, side, incoming=False):
            slot = (1, 0, 2)[side] if incoming else side
            if stage == P1:
                v = near[side] if incoming else me[0]
                return remote(one(v), one(v), *sem(P1, slot), to_near[side])
            if stage == P2:
                v = far[side] if incoming else me[1]
                return remote(line(v), line(v), *sem(P2, slot), to_far[side])
            v = far[2] if incoming else far[1 - side]
            part = pairs[0] if slot == 1 else pairs[1]
            return remote(line(v, part), line(v, part), *sem(H2, slot), to_far[side])

        def plane():
            src = g_ref.at[:, hi, core, :, lo]
            return remote(src, src, send.at[DD, b, 0], recv.at[DD, b, 0], sibling)

        return b, zb, copies, plane

    def from_sibling(i, odd):
        b = 2 * i + odd
        zb = (z + 15 - i) % 16 if odd else (z + i) % 16
        dst = g_ref.at[:, zb // 8, 1 - core, :, zb % 8]
        return remote(dst, dst, send.at[DD, b, 0], recv.at[DD, b, 0], sibling)

    def step(t, carry):
        @pl.when(t < 8)
        def _():
            for odd in range(2):
                b, zb, copies, _ = pieces(t, odd)

                def arrive():
                    z_copy(zb, b, 0).wait_recv()

                if odd:
                    arrive()
                else:
                    pl.when(t > 0)(arrive)

                @pl.when(t < 7 if odd else (t < 7) & (t > 0))
                def _():
                    z_copy(zb, b + 2, odd).start()

                for side in range(3):
                    copies(P1, side).start()

        @pl.when(t < 5)
        def _():
            for side in range(2):
                column(t, side).start()

        @pl.when(t == 5)
        def _():
            rows = e_ref.at[pl.ds(20 * core, RADIUS), centre, main]
            pltpu.make_async_copy(rows, rows, orecv.at[0]).wait()
            extra_beyond().wait_recv()
            for side in range(2):
                extra_column(OUTER, side).start()

        @pl.when((t == 5) | (t == 6))
        def _():
            for side in range(2):
                outer_column(t - 5, side).start()

        @pl.when((t >= 7) & (t < 10))
        def _():
            for side in range(2):
                column(t - 2, side).start()

        @pl.when((t >= 1) & (t < 9))
        def _():
            for odd in range(2):
                _, _, copies, _ = pieces(t - 1, odd)
                for side in range(3):
                    copies(P1, side, True).wait_recv()
                for side in range(2):
                    copies(P2, side).start()

        @pl.when((t >= 3) & (t < 11))
        def _():
            for odd in range(2):
                _, _, copies, _ = pieces(t - 3, odd)
                for side in range(2):
                    copies(P2, 1 - side, True).wait_recv()
                    copies(H2, side).start()

        @pl.when(t >= 5)
        def _():
            for odd in range(2):
                _, _, copies, plane = pieces(t - 5, odd)
                for side in range(2):
                    copies(H2, side, True).wait_recv()
                plane().start()

        @pl.when(t < 8)
        def _():
            build_rows(taps_ref, a_ref, t)

        return carry

    lax.fori_loop(0, 13, step, 0)

    for copy in own[1:]:
        copy.wait()

    def columns_in(n, carry):
        for side in range(2):
            column(n, side).wait_recv()
        return carry

    lax.fori_loop(0, 8, columns_in, 0)
    for side in range(2):
        extra_column(OWN, side).wait_recv()
    inner_rows().start()
    inner_extra().start()

    lanes = lax.broadcasted_iota(jnp.int32, (SPAN, 128), 1)

    def spread(row, part, at):
        e_ref[row, :, MAIN:] = jnp.where(lanes == at, x_ref[part].astype(F32), 0.0).astype(BF)

    def spread_own(r, carry):
        spread(r, OWN, r)
        return carry

    def features(pair, carry):
        stencil_rows(a_ref, e_ref, f_ref, pair)
        return carry

    lax.fori_loop(RADIUS, RADIUS + 16, spread_own, 0)
    lax.fori_loop(2, 6, features, 0)

    for side in range(2):
        for m in range(2):
            outer_column(m, side).wait_recv()
        extra_column(OUTER, side).wait_recv()
    inner_back = e_ref.at[pl.ds(20 - 20 * core, RADIUS), :, main]
    remote(inner_back, inner_back, xsend.at[5], xrecv.at[5], sibling).wait_recv()
    inner_extra().wait_recv()
    for q in range(RADIUS):
        spread(q, 1 + core, jnp.where(top, 7 - q, 16 + q))
        spread(20 + q, 2 - core, jnp.where(bottom, 19 - q, 4 + q))
    lax.fori_loop(0, 2, features, 0)
    lax.fori_loop(6, 8, features, 0)

    def wait_planes(i, carry):
        for odd in range(2):
            from_sibling(i, odd).wait_recv()
        return carry

    lax.fori_loop(0, 8, wait_planes, 0)

    def lay(n, carry):
        band, half = n // 2, n % 2
        rows = g_ref[band // 4, (band // 2) % 2, band % 2, pl.ds(half * 2, 2)]
        flat = rows.reshape(16, 48 * 128)
        wt_ref[pl.ds(pl.multiple_of(n * 16, 16), 16), :] = flat[:, :DEPTH]
        return carry

    lax.fori_loop(0, 32, lay, 0)

    def mix(n, carry):
        cols = pl.ds(pl.multiple_of(n * 256, 256), 256)
        total = lax.dot_general(
            f_ref[...], wt_ref[cols, :], (((1,), (1,)), ((), ())), preferred_element_type=F32
        )
        total = total + bias_ref[:, cols]
        value = 0.5 * total * (1.0 + lax.erf(total * math.sqrt(0.5)))
        out_ref[:, cols] = value.astype(BF)
        return carry

    lax.fori_loop(0, 2, mix, 0)

    def drain(i, carry):
        for odd in range(2):
            b, zb, copies, plane = pieces(i, odd)

            @pl.when((i >= 0) if odd else (i > 0))
            def _():
                z_copy(zb, b, 0).wait_send()

            for side in range(3):
                copies(P1, side).wait_send()
            for side in range(2):
                copies(P2, side).wait_send()
                copies(H2, side).wait_send()
            plane().wait_send()
        for side in range(2):
            column(i, side).wait_send()
        return carry

    lax.fori_loop(0, 8, drain, 0)
    for q in range(RADIUS):
        strip(q).wait_send()
    extra_beyond().wait_send()
    for side in range(2):
        for m in range(2):
            outer_column(m, side).wait_send()
        for part in (OWN, OUTER):
            extra_column(part, side).wait_send()
    inner_rows().wait_send()
    inner_extra().wait_send()


def body(latent, filters, widths, mix_weight, mix_bias):
    vmem = pl.BlockSpec(memory_space=pltpu.VMEM)
    packed, extra = pl.pallas_call(
        prepare_kernel,
        grid=(1,),
        out_shape=(jax.ShapeDtypeStruct((48, 128), BF), jax.ShapeDtypeStruct((16, 128), BF)),
        in_specs=[
            pl.BlockSpec((1, BASES, MAIN + 1), lambda i: (0, 0, 0)),
            pl.BlockSpec((16, 16, 128), lambda i: (0, 0, 5)),
        ],
        out_specs=(pl.BlockSpec((48, 128), lambda i: (0, 0)), pl.BlockSpec((16, 128), lambda i: (0, 0))),
        scratch_shapes=[pltpu.VMEM((48, 128), F32)],
        name="prepare",
    )(jnp.transpose(mix_weight, (2, 0, 1)), latent)
    dma = pltpu.SemaphoreType.DMA
    out = pl.pallas_call(
        main_kernel,
        out_shape=jax.ShapeDtypeStruct((256, 512), BF),
        in_specs=[vmem] * 6,
        out_specs=vmem,
        scratch_shapes=[
            pltpu.VMEM((4, 2, 2, 4, 8, 48, 128), BF),
            pltpu.VMEM((24, SPAN, MAIN + 128), BF),
            pltpu.VMEM((3, SPAN, 128), BF),
            pltpu.VMEM((BASES, 16, 2 * RADIUS + 1, 128), F32),
            pltpu.VMEM((8, 288, 512), BF),
            pltpu.VMEM((256, DEPTH), BF),
            pltpu.VMEM((512, DEPTH), BF),
            dma((5, 16, 3)),
            dma((5, 16, 3)),
            dma((10, 2)),
            dma((10, 2)),
            dma((7,)),
            dma((7,)),
            dma((RADIUS,)),
            dma((1,)),
            dma((3,)),
        ],
        compiler_params=pltpu.CompilerParams(
            collective_id=0, has_side_effects=True, vmem_limit_bytes=60 << 20
        ),
        name="sphere",
    )(packed, extra, latent, jnp.transpose(filters, (0, 2, 1, 3)), widths, mix_bias[None])
    return out.reshape(16, 16, 512)


def solution(mesh):
    placed = (
        P("lat", "lon", None),
        P(None, "lat", None, None),
        P("lat", None),
        P(None, None, ("lat", "lon")),
        P(),
    )
    return jax.shard_map(
        body, mesh=mesh, in_specs=placed, out_specs=P("lat", "lon", None), check_vma=False
    )
```

time: 100 us -> 76.5 us (0.77)
  the two profiles are of different devices: /device:TPU:32 before, /device:TPU:1 now
where the time goes in v2:
time: 76.5 us; the launch traced here: 76.3 us
  Pallas kernels  74.6 us (98%)
  local copies, waits for them, and re-layouts  1.67 us (2%)
    pallas_call x1, Pallas kernels, body(): pl.pallas_call(main_kernel, out_shape=jax.ShapeDtypeStruct((256, 512), BF...  73.1 us
    unnamed x1, local copies, waits for them, and re-layouts  1.67 us
    pallas_call x1, Pallas kernels, body(): pl.pallas_call(prepare_kernel, grid=(1,), out_shape=(jax.ShapeDtypeStruct...  1.55 us

profile of v2, /device:TPU:1, one launch (start us, length us, event | category | flops | bytes accessed | tf_op | source)
XLA Modules:
  0.0 76.3 jit_solution(2674459786355945872)
XLA Ops:
  0.0 1.5 %prepare.1 = (bf16[48,128]{1,0:T(8,128)(2,1)}, bf16[16,128]{1,0:T(8,128)(2,1)}) custom-call(bf16[1,9,641]{2,1,0:T(8,128)(2,1)} %bitcast.6, bf16[16,16,641]{2,1,0:T(8,128)(2,1)} %latent.1), custom_call_target="tpu_custom_call" | custom-call | tf_op jit(solution)/shard_map/prepare/pallas_call | solution.py:429
  1.5 73.1 %sphere.1 = bf16[256,512]{1,0:T(8,128)(2,1)} custom-call(bf16[48,128]{1,0:T(8,128)(2,1)} %get-tuple-element.7.w_in, bf16[16,128]{1,0:T(8,128)(2,1)} %get-tuple-element.8.extra, bf16[16,16,641]{2,1,0:T(8,128)(2,1)} %latent.1, bf16[9,9,16,33]{3,2,1,0:T(8,128)(2,1)} %bitcast.5, s32[16,9]{1,0:T(8,128)} %widths_ref.1, f32[1,512]{1,0:T(1,128)} %bitcast.7), custom_call_target="tpu_custom_call" | custom-call | tf_op jit(solution)/shard_map/sphere/pallas_call | solution.py:442
  74.7 1.7 %copy.7 = bf16[16,16,512]{2,1,0:T(8,128)(2,1)} copy(bf16[16,16,512]{2,1,0:T(8,128)(2,1)} %bitcast.4) | data formatting | bytes 524288

commit v3 on v2

v3 whole, which is shorter than its diff:
```python
import math

import jax
import jax.numpy as jnp
from jax import lax
from jax.experimental import pallas as pl
from jax.experimental.pallas import tpu as pltpu
from jax.sharding import PartitionSpec as P

RADIUS = 4
REACH = 16
BASES = 9
MAIN = 640
SPAN = 48
DEPTH = 46 * 128
MESH = pl.DeviceIdType.MESH
BF = jnp.bfloat16
F32 = jnp.float32

Z1, P1, P2, DD = range(4)
OWN, OUTER, INNER = range(3)
STRIPS_AT = 6
INNER_AT = 5


def device_of(x, y, z, core):
    return (x * 4 + (z // 8) * 2 + core, y * 8 + z % 8)


def prepare(w_ref, latent, packed_ref, extra_ref, rows_ref):
    w = w_ref[0].astype(F32)
    for t in range(5):
        rows_ref[t * BASES : (t + 1) * BASES, :] = w[:, t * 128 : (t + 1) * 128]
    lane = lax.broadcasted_iota(jnp.int32, (BASES, 128), 1)
    row = lax.broadcasted_iota(jnp.int32, (BASES, 128), 0)
    last = jnp.where(lane == row, jnp.broadcast_to(w[:, MAIN:], (BASES, 128)), 0.0)
    rows_ref[45:46, :] = jnp.sum(last, axis=0, keepdims=True)
    rows_ref[46:48, :] = jnp.zeros((2, 128), F32)
    packed_ref[...] = rows_ref[...].astype(BF)
    lane = lax.broadcasted_iota(jnp.int32, (16, 128), 1)
    extra = jnp.zeros((16, 128), F32)
    for r in range(16):
        column = latent[r, :, MAIN:].astype(F32)
        extra = jnp.where(lane == RADIUS + r, jnp.broadcast_to(column, (16, 128)), extra)
    extra_ref[...] = extra.astype(BF)


def mask_taps(filters_ref, widths_ref, taps_ref):
    lane = lax.broadcasted_iota(jnp.int32, (16, 128), 1)
    inside = [
        jnp.abs(lane - REACH) <= jnp.broadcast_to(widths_ref[:, d : d + 1], (16, 128))
        for d in range(2 * RADIUS + 1)
    ]
    for k in range(BASES):
        taps = filters_ref[k].astype(F32)
        taps = jnp.pad(taps, ((0, 0), (0, 0), (0, 128 - taps.shape[2])))
        taps = jnp.stack([jnp.where(inside[d], taps[d], 0.0) for d in range(2 * RADIUS + 1)])
        taps_ref[k] = jnp.transpose(taps, (1, 0, 2))


def build_rows(taps_ref, a_ref, pair):
    lane = lax.broadcasted_iota(jnp.int32, (16, 128), 1)
    zero = jnp.zeros((16, 128), F32)
    for s in range(2):
        i = pair * 2 + s
        for k in range(BASES):
            taps = taps_ref[k, i]
            tiles = [None] * 4

            def put(t, part):
                tiles[t] = part if tiles[t] is None else tiles[t] + part

            for d in range(2 * RADIUS + 1):
                first, at = divmod(SPAN * (d + s), 128)
                line = jnp.broadcast_to(taps[d : d + 1], (16, 128))
                line = pltpu.roll(line, at, 1, stride=1, stride_axis=0)
                if at + SPAN > 128:
                    put(first, jnp.where(lane >= at, line, zero))
                    put(first + 1, jnp.where(lane < at, line, zero))
                else:
                    put(first, line)
            rows = pl.ds((s * BASES + k) * 16, 16)
            a_ref[pair, rows, :] = jnp.concatenate(tiles, 1).astype(BF)


def stencil_rows(a_ref, e_ref, f_ref, pair):
    lane = lax.broadcasted_iota(jnp.int32, (16, 128), 1)
    slab = e_ref[pl.ds(pair * 2, 10)].reshape(10 * SPAN, MAIN + 128)
    found = jnp.dot(a_ref[pair][:, : 10 * SPAN], slab, preferred_element_type=F32)
    for s in range(2):
        rows = pl.ds(pl.multiple_of((pair * 2 + s) * 16, 16), 16)
        last = jnp.zeros((16, 128), F32)
        for k in range(BASES):
            part = found[(s * BASES + k) * 16 : (s * BASES + k + 1) * 16]
            for t in range(5):
                h = t * BASES + k
                f_ref[rows, h * 128 : (h + 1) * 128] = part[:, t * 128 : (t + 1) * 128].astype(BF)
            tail = jnp.sum(part[:, MAIN:], axis=1, keepdims=True)
            last = jnp.where(lane == k, jnp.broadcast_to(tail, (16, 128)), last)
        f_ref[rows, 45 * 128 :] = last.astype(BF)


def main_kernel(
    w_ref, latent, filters_ref, widths_ref, bias_ref, out_ref,
    w_in, extra, rows_ref, g_ref, e_ref, x_ref, taps_ref, a_ref, f_ref, wt_ref, perm_ref, value_ref,
    send, recv, csend, crecv, xsend, xrecv, osend, orecv, own_sem,
):
    lat, lon = lax.axis_index("lat"), lax.axis_index("lon")
    x, core = lat // 4, lat % 2
    y = lon // 8
    z = ((lat // 2) % 2) * 8 + lon % 8
    xs = ((x + 3) % 4, (x + 1) % 4, (x + 2) % 4)
    ys = ((y + 3) % 4, (y + 1) % 4, (y + 2) % 4)
    to_x = [device_of(v, y, z, core) for v in xs]
    to_y = [device_of(x, v, z, core) for v in ys]
    to_z = [[device_of(x, y, (z + 16 + d * n) % 16, core) for d in (-1, 1)] for n in range(1, 9)]
    sibling = (lat + 1 - 2 * core, lon)
    to_lon = [(lat, (lon + 31) % 32), (lat, (lon + 1) % 32)]
    top, bottom = lat == 0, lat == 15
    pole = top | bottom
    beyond = (
        jnp.where(pole, lat, lat - 1 + 2 * core),
        jnp.where(pole, (lon + 16) % 32, lon),
    )

    barrier = pltpu.get_barrier_semaphore()
    peers = to_x + to_y + sum(to_z[:7], []) + to_z[7][:1] + [sibling] + to_lon + [beyond]
    for peer in peers:
        pl.semaphore_signal(barrier, inc=1, device_id=peer, device_id_type=MESH)
    prepare(w_ref, latent, w_in, extra, rows_ref)
    mask_taps(filters_ref, widths_ref, taps_ref)
    pl.semaphore_wait(barrier, len(peers))

    def remote(src, dst, s, r, where):
        return pltpu.make_async_remote_copy(
            src_ref=src, dst_ref=dst, send_sem=s, recv_sem=r,
            device_id=where, device_id_type=MESH,
        )

    main = pl.ds(0, MAIN)
    centre = pl.ds(16, 16)

    def column(c, side):
        n = jnp.where(core == 0, 7 - c, c)
        rows = pl.ds(RADIUS + 2 * n, 2)
        dst = e_ref.at[rows, pl.ds(32 * (1 - side), 16), main]
        return remote(
            latent.at[pl.ds(2 * n, 2), :, main], dst,
            csend.at[c, side], crecv.at[c, side], to_lon[side],
        )

    def outer_column(m, side):
        rows = pl.ds(20 * core + 2 * m, 2)
        dst = e_ref.at[rows, pl.ds(32 * (1 - side), 16), main]
        return remote(
            e_ref.at[rows, centre, main], dst,
            csend.at[8 + m, side], crecv.at[8 + m, side], to_lon[side],
        )

    def strip(q):
        row = jnp.where(pole, jnp.where(core == 0, 3 - q, 23 - q), jnp.where(core == 0, 20 + q, q))
        return remote(
            latent.at[12 * core + q, :, main], e_ref.at[row, centre, main],
            osend.at[q], orecv.at[0], beyond,
        )

    def extra_beyond():
        return remote(extra, x_ref.at[OUTER, centre, :], xsend.at[2], xrecv.at[2], beyond)

    def extra_column(part, side):
        src = extra if part == OWN else x_ref.at[OUTER, centre, :]
        dst = x_ref.at[part, pl.ds(32 * (1 - side), 16), :]
        return remote(src, dst, xsend.at[3 * part + side], xrecv.at[3 * part + side], to_lon[side])

    def inner_rows():
        src = e_ref.at[pl.ds(16 - 12 * core, RADIUS), :, main]
        dst = e_ref.at[pl.ds(20 * core, RADIUS), :, main]
        return remote(src, dst, xsend.at[5], xrecv.at[5], sibling)

    def inner_extra():
        return remote(x_ref.at[OWN], x_ref.at[INNER], xsend.at[6], xrecv.at[6], sibling)

    def block(b):
        return g_ref.at[b, core, x, y]

    def z_copy(b, side, hops=1):
        return remote(w_in, block(b), send.at[Z1, b, 0], recv.at[Z1, b, 0], to_z[hops - 1][side])

    for hops in range(1, 9):
        for side in range(2):
            if hops < 8 or side == 1:
                z_copy(2 * hops - side, side, hops).start()
    own = [
        pltpu.make_async_copy(w_in, block(0), own_sem.at[0]),
        pltpu.make_async_copy(
            latent.at[:, :, main], e_ref.at[pl.ds(RADIUS, 16), centre, main], own_sem.at[1]
        ),
        pltpu.make_async_copy(extra, x_ref.at[OWN, centre, :], own_sem.at[2]),
    ]
    for copy in own:
        copy.start()
    own[0].wait()

    def pieces(i, odd):
        b = 2 * i + odd
        near, far = (ys, xs) if odd else (xs, ys)
        to_near, to_far = (to_y, to_x) if odd else (to_x, to_y)
        me = (y, x) if odd else (x, y)

        def one(v):
            return g_ref.at[b, core, x, v] if odd else g_ref.at[b, core, v, y]

        def line(v):
            return g_ref.at[b, core, v] if odd else g_ref.at[b, core, :, v]

        def sem(stage, slot):
            return send.at[stage, b, slot], recv.at[stage, b, slot]

        def copies(stage, side, incoming=False):
            slot = (1, 0, 2)[side] if incoming else side
            if stage == P1:
                v = near[side] if incoming else me[0]
                return remote(one(v), one(v), *sem(P1, slot), to_near[side])
            v = far[side] if incoming else me[1]
            return remote(line(v), line(v), *sem(P2, slot), to_far[side])

        def plane():
            src = g_ref.at[b, core]
            return remote(src, src, send.at[DD, b, 0], recv.at[DD, b, 0], sibling)

        return b, copies, plane

    def from_sibling(b):
        dst = g_ref.at[b, 1 - core]
        return remote(dst, dst, send.at[DD, b, 0], recv.at[DD, b, 0], sibling)

    def lay(b, c):
        flat = g_ref[b, c].reshape(16, 48 * 128)
        wt_ref[pl.ds(pl.multiple_of((b * 2 + c) * 16, 16), 16), :] = flat[:, :DEPTH]

    def planar(i, odd):
        _, copies, _ = pieces(i, odd)
        for side in range(3):
            copies(P1, side).start()

    planar(0, 0)
    for q in range(RADIUS):
        strip(q).start()
    extra_beyond().start()
    for side in range(2):
        extra_column(OWN, side).start()

    def every(c, carry):
        for side in range(2):
            column(c, side).start()
        return carry

    lax.fori_loop(0, 8, every, 0)

    def arrive(t, odd):
        z_copy(2 * t + odd, 0).wait_recv()
        planar(t, odd)

    def first(t, carry):
        pl.when(t > 0)(lambda: arrive(t, 0))
        arrive(t, 1)
        return carry

    def step(u, carry):
        @pl.when(u < 8)
        def _():
            for odd in range(2):
                _, copies, _ = pieces(u, odd)
                for side in range(3):
                    copies(P1, side, True).wait_recv()
                for side in range(3):
                    copies(P2, side).start()

        @pl.when(u < 4)
        def _():
            for odd in range(2):
                arrive(u + 4, odd)

        @pl.when(u == STRIPS_AT)
        def _():
            rows = e_ref.at[pl.ds(20 * core, RADIUS), centre, main]
            pltpu.make_async_copy(rows, rows, orecv.at[0]).wait()
            extra_beyond().wait_recv()
            for side in range(2):
                extra_column(OUTER, side).start()
                for m in range(2):
                    outer_column(m, side).start()

        @pl.when((u >= 2) & (u < 10))
        def _():
            for odd in range(2):
                b, copies, plane = pieces(u - 2, odd)
                for side in range(3):
                    copies(P2, side, True).wait_recv()
                plane().start()
                lay(b, core)

        @pl.when((u >= 3) & (u < 10))
        def _():
            for odd in range(2):
                b = 2 * (u - 3) + odd
                from_sibling(b).wait_recv()
                lay(b, 1 - core)

        @pl.when(u < 8)
        def _():
            build_rows(taps_ref, a_ref, u)

        @pl.when(u == INNER_AT)
        def _():
            own[1].wait()
            own[2].wait()
            for side in range(2):
                for c in range(2):
                    column(c, side).wait_recv()
                extra_column(OWN, side).wait_recv()
            inner_rows().start()
            inner_extra().start()

        @pl.when(u == 7)
        def _():
            inner_back = e_ref.at[pl.ds(20 - 20 * core, RADIUS), :, main]
            remote(inner_back, inner_back, xsend.at[5], xrecv.at[5], sibling).wait_recv()
            inner_extra().wait_recv()
            for q in range(RADIUS):
                top_lane = jnp.where(top, 7 - q, 16 + q)
                low_lane = jnp.where(bottom, 19 - q, 4 + q)
                spread(20 - 20 * core + q, INNER, jnp.where(core == 0, low_lane, top_lane))
            lax.fori_loop(RADIUS, RADIUS + 16, spread_own, 0)

        @pl.when((u >= 7) & (u < 10))
        def _():
            def early(k, c):
                n = 2 * (u - 7) + k
                for side in range(2):
                    column(n + 2, side).wait_recv()
                return features(n, c)

            lax.fori_loop(0, 2, early, 0)

        return carry

    lanes = lax.broadcasted_iota(jnp.int32, (SPAN, 128), 1)

    def spread(row, part, at):
        e_ref[row, :, MAIN:] = jnp.where(lanes == at, x_ref[part].astype(F32), 0.0).astype(BF)

    def spread_own(r, carry):
        spread(r, OWN, r)
        return carry

    def features(n, carry):
        stencil_rows(a_ref, e_ref, f_ref, jnp.where(core == 0, 7 - n, n))
        return carry

    def places(n, carry):
        i, odd, c = n // 4, (n // 2) % 2, n % 2
        place = jnp.where(odd == 1, z + 15 - i, z + i) % 16
        row = lax.broadcasted_iota(jnp.int32, (16, 512), 0)
        channel = lax.broadcasted_iota(jnp.int32, (16, 512), 1)
        at = (row >> 2) * 128 + (row & 3) * 8 + ((place // 8) * 64 + c * 32 + place % 8)
        perm_ref[pl.ds(pl.multiple_of(n * 16, 16), 16), :] = jnp.where(channel == at, 1.0, 0.0).astype(BF)
        return carry

    lax.fori_loop(0, 32, places, 0)

    lax.fori_loop(0, 4, first, 0)
    lax.fori_loop(0, 10, step, 0)

    for side in range(2):
        for m in range(2):
            outer_column(m, side).wait_recv()
        extra_column(OUTER, side).wait_recv()
    for q in range(RADIUS):
        top_lane = jnp.where(top, 7 - q, 16 + q)
        low_lane = jnp.where(bottom, 19 - q, 4 + q)
        spread(20 * core + q, OUTER, jnp.where(core == 0, top_lane, low_lane))
    lax.fori_loop(6, 8, features, 0)

    def mix(n, carry):
        @pl.when(n == 1)
        def _():
            for b in (14, 15):
                from_sibling(b).wait_recv()
                lay(b, 1 - core)

        cols = pl.ds(pl.multiple_of(n * 256, 256), 256)
        total = lax.dot_general(
            f_ref[...], wt_ref[cols, :], (((1,), (1,)), ((), ())), preferred_element_type=F32
        )
        bias = lax.dot_general(
            bias_ref[...], perm_ref[cols, :].astype(F32), (((1,), (1,)), ((), ())),
            precision=lax.Precision.HIGHEST, preferred_element_type=F32,
        )
        total = total + bias
        value = 0.5 * total * (1.0 + lax.erf(total * math.sqrt(0.5)))
        value_ref[:, cols] = value.astype(BF)
        return carry

    lax.fori_loop(0, 2, mix, 0)
    out_ref[...] = jnp.dot(
        value_ref[...], perm_ref[...], preferred_element_type=F32
    ).astype(BF)

    def drain(i, carry):
        for odd in range(2):
            b, copies, plane = pieces(i, odd)

            @pl.when((i >= 0) if odd else (i > 0))
            def _():
                z_copy(b, 0).wait_send()

            for side in range(3):
                copies(P1, side).wait_send()
                copies(P2, side).wait_send()
            plane().wait_send()
        for side in range(2):
            column(i, side).wait_send()
        return carry

    lax.fori_loop(0, 8, drain, 0)
    for q in range(RADIUS):
        strip(q).wait_send()
    extra_beyond().wait_send()
    for side in range(2):
        for m in range(2):
            outer_column(m, side).wait_send()
        for part in (OWN, OUTER):
            extra_column(part, side).wait_send()
    inner_rows().wait_send()
    inner_extra().wait_send()


def body(latent, filters, widths, mix_weight, mix_bias):
    vmem = pl.BlockSpec(memory_space=pltpu.VMEM)
    dma = pltpu.SemaphoreType.DMA
    out = pl.pallas_call(
        main_kernel,
        out_shape=jax.ShapeDtypeStruct((256, 512), BF),
        in_specs=[vmem] * 5,
        out_specs=vmem,
        scratch_shapes=[
            pltpu.VMEM((48, 128), BF),
            pltpu.VMEM((16, 128), BF),
            pltpu.VMEM((48, 128), F32),
            pltpu.VMEM((16, 2, 4, 4, 48, 128), BF),
            pltpu.VMEM((24, SPAN, MAIN + 128), BF),
            pltpu.VMEM((3, SPAN, 128), BF),
            pltpu.VMEM((BASES, 16, 2 * RADIUS + 1, 128), F32),
            pltpu.VMEM((8, 288, 512), BF),
            pltpu.VMEM((256, DEPTH), BF),
            pltpu.VMEM((512, DEPTH), BF),
            pltpu.VMEM((512, 512), BF),
            pltpu.VMEM((256, 512), BF),
            dma((4, 16, 3)),
            dma((4, 16, 3)),
            dma((10, 2)),
            dma((10, 2)),
            dma((7,)),
            dma((7,)),
            dma((RADIUS,)),
            dma((1,)),
            dma((3,)),
        ],
        compiler_params=pltpu.CompilerParams(
            collective_id=0, has_side_effects=True, vmem_limit_bytes=60 << 20
        ),
        name="sphere",
    )(
        jnp.transpose(mix_weight, (2, 0, 1)),
        latent,
        jnp.transpose(filters, (0, 2, 1, 3)),
        widths,
        mix_bias[None],
    )
    return out.reshape(16, 16, 512)


def solution(mesh):
    placed = (
        P("lat", "lon", None),
        P(None, "lat", None, None),
        P("lat", None),
        P(None, None, ("lat", "lon")),
        P(),
    )
    return jax.shard_map(
        body, mesh=mesh, in_specs=placed, out_specs=P("lat", "lon", None), check_vma=False
    )
```

time: 76.5 us -> 67.7 us (0.88)
  Pallas kernels: 74.6 us -> 65.6 us
    pallas_call x1, Pallas kernels: 73.1 us -> 65.6 us  [body(): pl.pallas_call(main_kernel, out_shape=jax.ShapeDtypeStruct((256, 512), BF...]
    pallas_call x1 -> x0, Pallas kernels: 1.55 us -> none  [body(): pl.pallas_call(prepare_kernel, grid=(1,), out_shape=(jax.ShapeDtypeStruct...]
where the time goes in v3:
time: 67.7 us; the launch traced here: 67.3 us
  Pallas kernels  65.6 us (97%)
  local copies, waits for them, and re-layouts  1.67 us (2%)
    pallas_call x1, Pallas kernels, body(): pl.pallas_call(main_kernel, out_shape=jax.ShapeDtypeStruct((256, 512), BF...  65.6 us
    unnamed x1, local copies, waits for them, and re-layouts  1.67 us

profile of v3, /device:TPU:1, one launch (start us, length us, event | category | flops | bytes accessed | tf_op | source)
XLA Modules:
  0.0 67.3 jit_solution(15174288804397283276)
XLA Ops:
  0.0 65.6 %sphere.1 = bf16[256,512]{1,0:T(8,128)(2,1)} custom-call(bf16[1,9,641]{2,1,0:T(8,128)(2,1)} %bitcast.6, bf16[16,16,641]{2,1,0:T(8,128)(2,1)} %latent.1, bf16[9,9,16,33]{3,2,1,0:T(8,128)(2,1)} %bitcast.5, s32[16,9]{1,0:T(8,128)} %widths_ref.1, f32[1,512]{1,0:T(1,128)} %bitcast.7), custom_call_target="tpu_custom_call" | custom-call | tf_op jit(solution)/shard_map/sphere/pallas_call | solution.py:442
  65.6 1.7 %copy.7 = bf16[16,16,512]{2,1,0:T(8,128)(2,1)} copy(bf16[16,16,512]{2,1,0:T(8,128)(2,1)} %bitcast.4) | data formatting | bytes 524288

commit v4 on v3

--- a/solution.py
+++ b/solution.py
@@ -244,18 +244,12 @@
             copies(P1, side).start()
 
     planar(0, 0)
-    for q in range(RADIUS):
-        strip(q).start()
-    extra_beyond().start()
-    for side in range(2):
-        extra_column(OWN, side).start()
 
     def every(c, carry):
         for side in range(2):
             column(c, side).start()
         return carry
 
-    lax.fori_loop(0, 8, every, 0)
 
     def arrive(t, odd):
         z_copy(2 * t + odd, 0).wait_recv()
@@ -369,7 +363,14 @@
 
     lax.fori_loop(0, 32, places, 0)
 
-    lax.fori_loop(0, 4, first, 0)
+    lax.fori_loop(0, 2, first, 0)
+    for q in range(RADIUS):
+        strip(q).start()
+    extra_beyond().start()
+    for side in range(2):
+        extra_column(OWN, side).start()
+    lax.fori_loop(0, 8, every, 0)
+    lax.fori_loop(2, 4, first, 0)
     lax.fori_loop(0, 10, step, 0)
 
     for side in range(2):
@@ -441,7 +442,7 @@
     dma = pltpu.SemaphoreType.DMA
     out = pl.pallas_call(
         main_kernel,
-        out_shape=jax.ShapeDtypeStruct((256, 512), BF),
+        out_shape=pltpu.VMEM((256, 512), BF),
         in_specs=[vmem] * 5,
         out_specs=vmem,
         scratch_shapes=[

time: 67.7 us -> 66 us (0.975)
  local copies, waits for them, and re-layouts: 1.67 us -> 0.71 us
    unnamed x1, local copies, waits for them, and re-layouts: 1.67 us -> 0.71 us
where the time goes in v4:
time: 66 us; the launch traced here: 65.8 us
  Pallas kernels  65.1 us (99%)
  local copies, waits for them, and re-layouts  0.71 us (1%)
    pallas_call x1, Pallas kernels, body(): pl.pallas_call(main_kernel, out_shape=pltpu.VMEM((256, 512), BF), in_spec...  65.1 us

profile of v4, /device:TPU:1, one launch (start us, length us, event | category | flops | bytes accessed | tf_op | source)
XLA Modules:
  0.0 65.8 jit_solution(17014478867650784586)
XLA Ops:
  0.0 65.1 %sphere.1 = bf16[256,512]{1,0:T(8,128)(2,1)S(1)} custom-call(bf16[1,9,641]{2,1,0:T(8,128)(2,1)} %bitcast.6, bf16[16,16,641]{2,1,0:T(8,128)(2,1)} %latent.1, bf16[9,9,16,33]{3,2,1,0:T(8,128)(2,1)} %bitcast.5, s32[16,9]{1,0:T(8,128)} %widths_ref.1, f32[1,512]{1,0:T(1,128)} %bitcast.7), custom_call_target="tpu_custom_call" | custom-call | tf_op jit(solution)/shard_map/sphere/pallas_call | solution.py:443
  65.1 0.7 %copy.7 = bf16[16,16,512]{2,1,0:T(8,128)(2,1)} copy(bf16[16,16,512]{2,1,0:T(8,128)(2,1)S(1)} %bitcast.4) | data formatting | bytes 524288

commit v5 on v4

--- a/solution.py
+++ b/solution.py
@@ -102,7 +102,7 @@
 
 def main_kernel(
     w_ref, latent, filters_ref, widths_ref, bias_ref, out_ref,
-    w_in, extra, rows_ref, g_ref, e_ref, x_ref, taps_ref, a_ref, f_ref, wt_ref, perm_ref, value_ref,
+    w_in, extra, rows_ref, g_ref, e_ref, x_ref, taps_ref, a_ref, f_ref, wt_ref, perm_ref, value_ref, shift_ref,
     send, recv, csend, crecv, xsend, xrecv, osend, orecv, own_sem,
 ):
     lat, lon = lax.axis_index("lat"), lax.axis_index("lon")
@@ -362,6 +362,12 @@
         return carry
 
     lax.fori_loop(0, 32, places, 0)
+    for n in range(2):
+        cols = pl.ds(n * 256, 256)
+        shift_ref[:, cols] = lax.dot_general(
+            bias_ref[...], perm_ref[cols, :].astype(F32), (((1,), (1,)), ((), ())),
+            precision=lax.Precision.HIGHEST, preferred_element_type=F32,
+        )
 
     lax.fori_loop(0, 2, first, 0)
     for q in range(RADIUS):
@@ -394,11 +400,7 @@
         total = lax.dot_general(
             f_ref[...], wt_ref[cols, :], (((1,), (1,)), ((), ())), preferred_element_type=F32
         )
-        bias = lax.dot_general(
-            bias_ref[...], perm_ref[cols, :].astype(F32), (((1,), (1,)), ((), ())),
-            precision=lax.Precision.HIGHEST, preferred_element_type=F32,
-        )
-        total = total + bias
+        total = total + shift_ref[:, cols]
         value = 0.5 * total * (1.0 + lax.erf(total * math.sqrt(0.5)))
         value_ref[:, cols] = value.astype(BF)
         return carry
@@ -458,6 +460,7 @@
             pltpu.VMEM((512, DEPTH), BF),
             pltpu.VMEM((512, 512), BF),
             pltpu.VMEM((256, 512), BF),
+            pltpu.VMEM((1, 512), F32),
             dma((4, 16, 3)),
             dma((4, 16, 3)),
             dma((10, 2)),

time: 66 us -> 65.2 us (0.988)
  Pallas kernels: 65.1 us -> 64.3 us
    pallas_call x1, Pallas kernels: 65.1 us -> 64.3 us  [body(): pl.pallas_call(main_kernel, out_shape=pltpu.VMEM((256, 512), BF), in_spec...]
where the time goes in v5:
time: 65.2 us; the launch traced here: 65 us
  Pallas kernels  64.3 us (99%)
  local copies, waits for them, and re-layouts  0.71 us (1%)
    pallas_call x1, Pallas kernels, body(): pl.pallas_call(main_kernel, out_shape=pltpu.VMEM((256, 512), BF), in_spec...  64.3 us

profile of v5, /device:TPU:1, one launch (start us, length us, event | category | flops | bytes accessed | tf_op | source)
XLA Modules:
  0.0 65.0 jit_solution(14069950251210161976)
XLA Ops:
  0.0 64.3 %sphere.1 = bf16[256,512]{1,0:T(8,128)(2,1)S(1)} custom-call(bf16[1,9,641]{2,1,0:T(8,128)(2,1)} %bitcast.6, bf16[16,16,641]{2,1,0:T(8,128)(2,1)} %latent.1, bf16[9,9,16,33]{3,2,1,0:T(8,128)(2,1)} %bitcast.5, s32[16,9]{1,0:T(8,128)} %widths_ref.1, f32[1,512]{1,0:T(1,128)} %bitcast.7), custom_call_target="tpu_custom_call" | custom-call | tf_op jit(solution)/shard_map/sphere/pallas_call | solution.py:445
  64.3 0.7 %copy.7 = bf16[16,16,512]{2,1,0:T(8,128)(2,1)} copy(bf16[16,16,512]{2,1,0:T(8,128)(2,1)S(1)} %bitcast.4) | data formatting | bytes 524288
